TPU v7x, 128 devices: a whole 4x4x4 slice. The times are simulated.
128 devices in a mesh: joined: 8 (over z, core), view: 16 (over y, x).
Axes of the slice: x: 4, y: 4, z: 4, core: 2. Of those that a mesh axis runs over, the one named last changes fastest.
Arguments:
- estimate: float32 [16, 1024, 2048], P('view', 'joined'), may hold values from 0.5 to 2
- views: float32 [16, 8, 1024, 2048], P('view', None, 'joined'), may hold values from 0.25 to 4
- psf: float32 [8, 2, 65], replicated, may hold values from 0.2 to 2
- offsets: int32 [8, 2], replicated, may hold values from -16 to 16, as said below
- lengths: int32 [8, 2], replicated, may hold values from 1 to 8, as said below
Outputs:
- deconvolved: float32 [16, 1024, 2048], P('view', 'joined')
Inputs may be any that keep to these rules, and one draw needn't show every extreme that they name: `offsets`: offsets along each lateral dimension reach both -16 and 16 in every draw. `lengths`: in every depth block some view has all 8 planes.
All inputs are finite; a program needn't handle non-finite values.
Results may differ from a plain program's by a relative error of at most 0.0001.
Values sent between devices are 32-bit elements; how exact they have to be, the bound alone decides.
A program may use at most 128 MiB of HBM per device.

v0:
```python
import jax
import jax.numpy as jnp
from jax import lax
from jax.sharding import PartitionSpec as P

MAXD = 16
BLOCKS = 2
YBLOCK = 128


def padded_2(value, sides, width):
    for axis, dim in sides:
        peers, length = (lax.axis_size(axis), value.shape[dim])
        up = [(i, (i + 1) % peers) for i in range(peers)]
        down = [(j, i) for i, j in up]
        last = lax.slice_in_dim(value, length - width, length, axis=dim)
        first = lax.slice_in_dim(value, 0, width, axis=dim)
        before = lax.ppermute(last, axis, up)
        after = lax.ppermute(first, axis, down)
        value = jnp.concatenate([before, value, after], axis=dim)
    return value


def spread_taps(offset, kernel):
    tap_range = jnp.arange(kernel.shape[0], dtype=jnp.int32)
    onehot = (offset[:, :, None] == tap_range[None, None, :]).astype(jnp.float32)
    return jnp.einsum("ijt,t->ij", onehot, kernel, precision=lax.Precision.HIGHEST)


def blur_lateral(field, shift, band, radius, margin):
    depth_rows = field.shape[0]
    tile_rows = field.shape[1]
    lateral_cols = field.shape[2]
    block_cols = band.shape[1]
    block_total = lateral_cols // block_cols
    wrapped = jnp.concatenate(
        [field[:, :, lateral_cols - margin :], field, field[:, :, :margin]], axis=2
    )
    window = lax.dynamic_slice_in_dim(
        wrapped, margin + shift - radius, lateral_cols + 2 * radius, 2
    )
    leading = window[:, :, :lateral_cols].reshape(depth_rows, tile_rows, block_total, block_cols)
    trailing = jnp.concatenate(
        [
            window[:, :, block_cols:],
            jnp.zeros((depth_rows, tile_rows, block_cols - 2 * radius), jnp.float32),
        ],
        axis=2,
    )
    trailing = trailing.reshape(depth_rows, tile_rows, block_total, block_cols)[
        :, :, :, : 2 * radius
    ]
    stacked = jnp.concatenate([leading, trailing], axis=3)
    result = jnp.einsum("zxje,et->zxjt", stacked, band, precision=lax.Precision.HIGHEST)
    return result.reshape(depth_rows, tile_rows, lateral_cols)


def per_device(estimate, views, psf, offsets, lengths):
    owned_rows = estimate.shape[0]
    position = lax.axis_index("view")
    member = position // BLOCKS
    block = position % BLOCKS
    radius = (psf.shape[2] - 1) // 2
    margin = radius + MAXD
    plane_count = views.shape[1]
    tile_cols = views.shape[2]
    lateral_cols = views.shape[3]
    extended = tile_cols + 2 * radius
    widened = YBLOCK + 2 * radius
    highest = lax.Precision.HIGHEST
    kernels = lax.dynamic_index_in_dim(psf, member, 0, keepdims=False)
    kernels = kernels / jnp.sum(kernels, axis=1, keepdims=True)
    shifts = lax.dynamic_index_in_dim(offsets, member, 0, keepdims=False)
    shift_x = shifts[0]
    shift_y = shifts[1]
    member_lengths = lax.dynamic_index_in_dim(lengths, member, 0, keepdims=False)
    own_length = lax.dynamic_index_in_dim(member_lengths, block, 0, keepdims=False)
    band_diff = lax.broadcasted_iota(jnp.int32, (extended, tile_cols), 0) - lax.broadcasted_iota(
        jnp.int32, (extended, tile_cols), 1
    )
    band_forward = spread_taps(band_diff, kernels[0])
    band_back = spread_taps(band_diff, kernels[0][::-1])
    block_diff = lax.broadcasted_iota(jnp.int32, (widened, YBLOCK), 0) - lax.broadcasted_iota(
        jnp.int32, (widened, YBLOCK), 1
    )
    lateral_forward = spread_taps(block_diff, kernels[1])
    lateral_back = spread_taps(block_diff, kernels[1][::-1])
    planes = jnp.arange(plane_count, dtype=jnp.int32)
    live = (planes < own_length).astype(jnp.float32)[:, None, None]
    observed = views[0] * live
    owned_planes = position * owned_rows + jnp.arange(owned_rows, dtype=jnp.int32)
    plane_block = owned_planes // plane_count
    plane_row = owned_planes % plane_count
    block_select = (plane_block[None, :] == jnp.arange(BLOCKS, dtype=jnp.int32)[:, None]).astype(
        jnp.float32
    )
    reached = (plane_row[None, None, :] < lengths[:, :, None]).astype(jnp.float32)
    counts = jnp.sum(reached * block_select[None, :, :], axis=(0, 1))
    current = estimate
    whole = lax.all_gather(current, "view", axis=0, tiled=True)
    mine = lax.dynamic_slice_in_dim(whole, block * plane_count, plane_count, 0)
    padded = padded_2(mine, (("joined", 1),), margin)
    window = lax.dynamic_slice_in_dim(padded, margin + shift_x - radius, extended, 1)
    blurred = jnp.einsum("zey,et->zty", window, band_forward, precision=highest)
    image = blur_lateral(blurred, shift_y, lateral_forward, radius, margin)
    ratio = observed / image
    ratio_padded = padded_2(ratio, (("joined", 1),), margin)
    window = lax.dynamic_slice_in_dim(ratio_padded, margin - shift_x - radius, extended, 1)
    spread_x = jnp.einsum("zey,et->zty", window, band_back, precision=highest)
    correction = blur_lateral(spread_x, -shift_y, lateral_back, radius, margin)
    selector = (jnp.arange(BLOCKS, dtype=jnp.int32) == block).astype(jnp.float32)[
        :, None, None, None
    ]
    placed = (selector * correction[None]).reshape(BLOCKS * plane_count, tile_cols, lateral_cols)
    total = lax.psum_scatter(placed, "view", scatter_dimension=0, tiled=True)
    current = current * total / counts[:, None, None]
    return current


def solution(mesh):
    return jax.shard_map(
        per_device,
        mesh=mesh,
        in_specs=(P("view", "joined", None), P("view", None, "joined", None), P(), P(), P()),
        out_specs=P("view", "joined", None),
        check_vma=False,
    )
```

profile of v0, /device:TPU:24, one launch (start us, length us, event | category | flops | bytes accessed | tf_op | source)
XLA Modules:
  0.0 536.8 jit_solution(9204132740623171197)
XLA Ops:
  6.5 0.7 all-gather.2.cloned.1.call-update
  7.3 115.3 %all-gather.2.cloned.1.call-done = f32[16,128,2048]{2,1,0:T(8,128)} async-done(((f32[1,128,2048]{2,1,0:T(8,128)}), f32[16,128,2048]{2,1,0:T(8,128)}) %all-gather.2.cloned.1.call-update) | async-done | bytes 16777232 | tf_op jit(solution)/shard_map/all_gather | solution.py:100
  122.6 5.2 constant_dynamic-slice_fusion
  127.8 3.0 collective-permute-start.1
  130.8 0.8 fusion.34
  131.6 0.6 fusion.48
  134.8 0.6 dynamic_slice.29
  135.4 0.6 compare_convert_fusion.1
  136.0 0.8 bitcast_divide_fusion
  136.8 0.8 iota_compare_fusion
  137.6 2.9 fusion.27
  140.6 2.9 fusion.25
  143.5 7.7 %constant_dynamic-slice_fusion.7 = f32[8,128,2048]{2,1,0:T(8,128)} fusion(f32[16,128,2048]{2,1,0:T(8,128)} %all-gather.2.cloned.1.call-done, s32[]{:T(128)S(6)} %select_n.58), kind=kLoop, calls=%fused_computation.45 | loop fusion | bytes 16777220 | tf_op jit(solution)/shard_map/dynamic_slice | solution.py:101
  151.2 14.8 %collective-permute-done = f32[8,48,2048]{2,1,0:T(8,128)} collective-permute-done((f32[8,48,2048]{2,1,0:T(8,128)}, f32[8,48,2048]{2,1,0:T(8,128)}, u32[]{:S(2)}, u32[]{:S(2)}) %collective-permute-start) | collective-permute-done | bytes 3145760 | tf_op jit(solution)/shard_map/ppermute | solution.py:18
  166.0 15.3 %fusion.17 = f32[8,128,2048]{2,1,0:T(8,128)S(1)} fusion(f32[192,128,1]{1,0,2:T(8,128)S(1)} %bitcast.80, s32[]{:T(128)S(6)} %select_n.59, f32[8,48,2048]{2,1,0:T(8,128)} %collective-permute-done, f32[8,128,2048]{2,1,0:T(8,128)} %constant_dynamic-slice_fusion.7, f32[8,48,2048]{2,1,0:T(8,128)} %collective-permute-done.1), kind=kOutput, calls=%fused_computation.24 | convolution fusion | flops 4838129664 | bytes 23166980 | tf_op jit(solution)/shard_map/zey,et->zty/dot_general | solution.py:104
  181.3 3.2 copy-done.5
  184.6 0.2 fusion.47
  184.8 11.3 %concatenate.25 = f32[8,128,2144]{2,1,0:T(8,128)} concatenate(f32[8,128,48]{2,1,0:T(8,128)S(1)} %get-tuple-element.12, f32[8,128,2048]{2,1,0:T(8,128)} %copy-done.5, f32[8,128,48]{2,1,0:T(8,128)S(1)} %get-tuple-element.11), dimensions={2} | concatenate | bytes 17563648 | tf_op jit(solution)/shard_map/concatenate | solution.py:36
  196.1 9.2 %constant_dynamic-slice_fusion.5 = f32[8,128,2048]{2,1,0:T(8,128)} fusion(f32[8,128,2144]{2,1,0:T(8,128)} %concatenate.25, s32[]{:T(128)S(6)} %select_n.60), kind=kLoop, calls=%fused_computation.43 | loop fusion | bytes 16777220 | tf_op jit(solution)/shard_map/slice | solution.py:42
  205.3 5.5 %constant_dynamic-slice_fusion.4 = f32[8,128,1984]{2,1,0:T(8,128)} fusion(f32[8,128,2144]{2,1,0:T(8,128)S(1)} %copy-done.2, s32[]{:T(128)S(6)} %add.101), kind=kLoop, calls=%fused_computation.42 | loop fusion | bytes 16252932 | tf_op jit(solution)/shard_map/slice | solution.py:45
  210.7 9.1 %copy.35 = f32[8,128,1984]{1,2,0:T(8,128)} copy(f32[8,128,1984]{2,1,0:T(8,128)} %constant_dynamic-slice_fusion.4) | data formatting | bytes 16252928
  219.8 4.0 concatenate.26.clone
  223.8 2.5 slice.78
  226.3 9.6 %copy.31 = f32[8,128,2048]{1,2,0:T(8,128)} copy(f32[8,128,2048]{2,1,0:T(8,128)} %constant_dynamic-slice_fusion.5) | data formatting | bytes 16777216 | tf_op jit(solution)/shard_map/reshape | solution.py:42
  235.8 13.7 %fusion.8 = f32[8,128,16,128]{1,3,2,0:T(8,128)} fusion(f32[192,128,1,1]{1,0,3,2:T(8,128)S(1)} %bitcast.77, f32[8,128,16,64]{1,3,2,0:T(8,128)} %slice.78, f32[8,128,16,128]{1,3,2,0:T(8,128)} %bitcast.71), kind=kOutput, calls=%fused_computation.13 | convolution fusion | flops 4834983936 | bytes 21069824 | tf_op jit(solution)/shard_map/zxje,et->zxjt/dot_general | solution.py:54
  249.6 9.2 %copy.20 = f32[8,128,2048]{2,1,0:T(8,128)} copy(f32[8,128,2048]{1,2,0:T(8,128)} %bitcast.72) | data formatting | bytes 16777216 | tf_op jit(solution)/shard_map/reshape | solution.py:55
  258.8 11.9 %fusion.16 = f32[8,128,2048]{2,1,0:T(8,128)} fusion(f32[8,128,2048]{2,1,0:T(8,128)} %copy.20, f32[1,8,128,2048]{3,2,1,0:T(8,128)} %param.6, f32[8]{0:T(128)S(1)} %compare_convert_fusion.1), kind=kLoop, calls=%fused_computation.22 | loop fusion | flops 4194304 | bytes 25165856 | tf_op jit(solution)/shard_map/div | solution.py:106
  270.8 5.2 fusion.46
  275.9 0.2 collective-permute-start.2
  276.2 2.7 collective-permute-start.3
  281.1 3.9 fusion.29
  285.0 3.8 fusion.23
  288.8 25.4 %collective-permute-done.2 = f32[8,48,2048]{2,1,0:T(8,128)} collective-permute-done((f32[8,48,2048]{2,1,0:T(8,128)}, f32[8,48,2048]{2,1,0:T(8,128)}, u32[]{:S(2)}, u32[]{:S(2)}) %collective-permute-start.2) | collective-permute-done | bytes 3145760 | tf_op jit(solution)/shard_map/ppermute | solution.py:18
  314.2 15.4 %fusion.20 = f32[8,128,2048]{2,1,0:T(8,128)} fusion(f32[192,128,1]{1,0,2:T(8,128)S(1)} %bitcast.79, s32[]{:T(128)S(6)} %select_n.61, f32[8,48,2048]{2,1,0:T(8,128)} %collective-permute-done.2, f32[8,128,2048]{2,1,0:T(8,128)S(1)} %copy-done.4, f32[8,48,2048]{2,1,0:T(8,128)} %collective-permute-done.3), kind=kOutput, calls=%fused_computation.25 | convolution fusion | flops 4838129664 | bytes 23166980 | tf_op jit(solution)/shard_map/zey,et->zty/dot_general | solution.py:109
  329.6 1.4 fusion.45
  331.0 11.3 %concatenate.29 = f32[8,128,2144]{2,1,0:T(8,128)} concatenate(f32[8,128,48]{2,1,0:T(8,128)S(1)} %get-tuple-element.8, f32[8,128,2048]{2,1,0:T(8,128)} %fusion.20, f32[8,128,48]{2,1,0:T(8,128)S(1)} %get-tuple-element.7), dimensions={2} | concatenate | bytes 17563648 | tf_op jit(solution)/shard_map/concatenate | solution.py:36
  342.3 9.2 %constant_dynamic-slice_fusion.3 = f32[8,128,2048]{2,1,0:T(8,128)} fusion(f32[8,128,2144]{2,1,0:T(8,128)} %concatenate.29, s32[]{:T(128)S(6)} %select_n.62), kind=kLoop, calls=%fused_computation.41 | loop fusion | bytes 16777220 | tf_op jit(solution)/shard_map/slice | solution.py:42
  351.5 5.5 %constant_dynamic-slice_fusion.2 = f32[8,128,1984]{2,1,0:T(8,128)} fusion(f32[8,128,2144]{2,1,0:T(8,128)S(1)} %copy-done.3, s32[]{:T(128)S(6)} %add.102), kind=kLoop, calls=%fused_computation.40 | loop fusion | bytes 16252932 | tf_op jit(solution)/shard_map/slice | solution.py:45
  356.9 9.1 %copy.36 = f32[8,128,1984]{1,2,0:T(8,128)} copy(f32[8,128,1984]{2,1,0:T(8,128)} %constant_dynamic-slice_fusion.2) | data formatting | bytes 16252928
  366.0 4.0 concatenate.30.clone
  370.0 2.5 slice.83
  372.5 9.4 %copy.33 = f32[8,128,2048]{1,2,0:T(8,128)} copy(f32[8,128,2048]{2,1,0:T(8,128)} %constant_dynamic-slice_fusion.3) | data formatting | bytes 16777216 | tf_op jit(solution)/shard_map/reshape | solution.py:42
  381.8 13.7 %fusion.12 = f32[8,128,16,128]{1,3,2,0:T(8,128)} fusion(f32[192,128,1,1]{1,0,3,2:T(8,128)S(1)} %bitcast.78, f32[8,128,16,64]{1,3,2,0:T(8,128)} %slice.83, f32[8,128,16,128]{1,3,2,0:T(8,128)} %bitcast.73), kind=kOutput, calls=%fused_computation.17 | convolution fusion | flops 4834983936 | bytes 21069824 | tf_op jit(solution)/shard_map/zxje,et->zxjt/dot_general | solution.py:54
  395.6 9.2 %copy.23 = f32[8,128,2048]{2,1,0:T(8,128)} copy(f32[8,128,2048]{1,2,0:T(8,128)} %bitcast.74) | data formatting | bytes 16777216 | tf_op jit(solution)/shard_map/mul | solution.py:114
  404.8 12.1 %bitcast_multiply_fusion = f32[16,128,2048]{2,1,0:T(8,128)} fusion(f32[8,128,2048]{2,1,0:T(8,128)} %copy.23, f32[16]{0:T(128)S(1)} %mul.45), kind=kLoop, calls=%fused_computation | loop fusion | flops 4194304 | bytes 25165888 | tf_op jit(solution)/shard_map/mul | solution.py:114
  417.0 0.7 fusion.33
  417.7 109.0 %reduce-scatter.4.cloned.1.call-done = f32[1,128,2048]{2,1,0:T(8,128)} async-done(((f32[16,128,2048]{2,1,0:T(8,128)}), f32[1,128,2048]{2,1,0:T(8,128)}) %reduce-scatter.4.cloned.1.call-update) | async-done | bytes 1048592
  526.7 3.0 multiply_divide_fusion
  (32 shorter events, 0.5 us)
Async XLA Ops:
  6.5 125.0 %copy-start = (s32[8,2]{0,1:T(2,128)S(1)}, s32[8,2]{0,1:T(2,128)}, u32[]{:S(2)}) copy-start(s32[8,2]{0,1:T(2,128)} %param.8) | copy-start | bytes 196
  6.5 128.2 %copy-start.8 = (s32[8,2]{0,1:T(2,128)S(1)}, s32[8,2]{0,1:T(2,128)}, u32[]{:S(2)}) copy-start(s32[8,2]{0,1:T(2,128)} %param.9) | copy-start | bytes 196
  6.5 116.1 %all-gather.2.cloned.1.call-start = ((), (), s32[]{:S(2)}) async-start(), calls=%async_computation.1 | async-start | bytes 17825792 | tf_op jit(solution)/shard_map/all_gather | solution.py:100
  7.3 519.4 %reduce-scatter.4.cloned.1.call-start = ((), (), s32[]{:S(2)}) async-start(), calls=%async_computation.2 | async-start | bytes 17825792
  127.8 38.2 %collective-permute-start = (f32[8,48,2048]{2,1,0:T(8,128)}, f32[8,48,2048]{2,1,0:T(8,128)}, u32[]{:S(2)}, u32[]{:S(2)}) collective-permute-start(f32[8,48,2048]{2,1,0:T(8,128)} %get-tuple-element.6), channel_id=1, source_target_pairs={{0,16},{16,32},{32,48},{48,64},{64,80},{80,96},{96,112},{112,0},{1... | collective-permute-start | bytes 9437192 | tf_op jit(solution)/shard_map/ppermute | solution.py:18
  127.8 38.2 %collective-permute-start.1 = (f32[8,48,2048]{2,1,0:T(8,128)S(1)}, f32[8,48,2048]{2,1,0:T(8,128)}, u32[]{:S(2)}, u32[]{:S(2)}) collective-permute-start(f32[8,48,2048]{2,1,0:T(8,128)S(1)} %get-tuple-element.5), channel_id=1, source_target_pairs={{16,0},{32,16},{48,32},{64,48},{80,64},{96,80},{112,96},{0,112},{1... | collective-permute-start | bytes 9437192 | tf_op jit(solution)/shard_map/ppermute | solution.py:19
  137.6 3.0 copy-start.7
  181.3 3.3 copy-start.5
  196.1 9.2 %copy-start.2 = (f32[8,128,2144]{2,1,0:T(8,128)S(1)}, f32[8,128,2144]{2,1,0:T(8,128)}, u32[]{:S(2)}) copy-start(f32[8,128,2144]{2,1,0:T(8,128)} %concatenate.25) | copy-start | bytes 26345476
  275.9 38.2 %collective-permute-start.2 = (f32[8,48,2048]{2,1,0:T(8,128)}, f32[8,48,2048]{2,1,0:T(8,128)}, u32[]{:S(2)}, u32[]{:S(2)}) collective-permute-start(f32[8,48,2048]{2,1,0:T(8,128)} %get-tuple-element.10), channel_id=1, source_target_pairs={{0,16},{16,32},{32,48},{48,64},{64,80},{80,96},{96,112},{112,0},{1... | collective-permute-start | bytes 9437192 | tf_op jit(solution)/shard_map/ppermute | solution.py:18
  276.2 38.0 %collective-permute-start.3 = (f32[8,48,2048]{2,1,0:T(8,128)S(1)}, f32[8,48,2048]{2,1,0:T(8,128)}, u32[]{:S(2)}, u32[]{:S(2)}) collective-permute-start(f32[8,48,2048]{2,1,0:T(8,128)S(1)} %get-tuple-element.9), channel_id=1, source_target_pairs={{16,0},{32,16},{48,32},{64,48},{80,64},{96,80},{112,96},{0,112},{1... | collective-permute-start | bytes 9437192 | tf_op jit(solution)/shard_map/ppermute | solution.py:19
  281.1 33.1 %copy-start.4 = (f32[8,128,2048]{2,1,0:T(8,128)S(1)}, f32[8,128,2048]{2,1,0:T(8,128)}, u32[]{:S(2)}) copy-start(f32[8,128,2048]{2,1,0:T(8,128)} %fusion.16) | copy-start | bytes 25165828
  342.3 9.2 %copy-start.3 = (f32[8,128,2144]{2,1,0:T(8,128)S(1)}, f32[8,128,2144]{2,1,0:T(8,128)}, u32[]{:S(2)}) copy-start(f32[8,128,2144]{2,1,0:T(8,128)} %concatenate.29) | copy-start | bytes 26345476
  416.9 112.8 %copy-start.1 = (s32[8,2]{0,1:T(2,128)S(1)}, s32[8,2]{0,1:T(2,128)}, u32[]{:S(2)}) copy-start(s32[8,2]{0,1:T(2,128)} %param.8) | copy-start | bytes 196
  416.9 109.8 %copy-start.6 = (f32[1,128,2048]{2,1,0:T(8,128)S(1)}, f32[1,128,2048]{2,1,0:T(8,128)}, u32[]{:S(2)}) copy-start(f32[1,128,2048]{2,1,0:T(8,128)} %param.5) | copy-start | bytes 3145732
Sparse Core Ops, SparseCore 0:
  9.5 113.1 all-gather.1
  417.1 109.5 reduce-scatter.3
where the time goes:
time: 546 us; the launch traced here: 537 us
  waiting for transfers between devices  265 us (49%)
  local copies, waits for them, and re-layouts  145 us (27%)
  matrix products  71.7 us (13%)
  other arithmetic  30.8 us (6%)
  between operations  18.1 us (3%)
  starting transfers between devices  5.95 us (1%)
    all_gather x1, waiting for transfers between devices, per_device(): whole = lax.all_gather(current, 'view', axis=0, tiled=True)  115 us
    unnamed x3, waiting for transfers between devices  110 us
    ppermute x2, waiting for transfers between devices, padded_2(): before = lax.ppermute(last, axis, up)  40.2 us
    dot_general x2, matrix products, blur_lateral(): jnp.einsum('zxje,et->zxjt', stacked, band, precision=lax.Precision.HIGHEST)  27.5 us
    concatenate x2, local copies, waits for them, and re-layouts, blur_lateral(): jnp.concatenate([field[:, :, lateral_cols - margin:], field, field[:, :,...  22.6 us
    unnamed x20, local copies, waits for them, and re-layouts  21.4 us
    reshape x2, local copies, waits for them, and re-layouts, blur_lateral(): window[:, :, :lateral_cols]  18.9 us
    slice x2, local copies, waits for them, and re-layouts, blur_lateral(): window[:, :, :lateral_cols]  18.3 us
  transfers between devices with their start and end apart: 6, of which 4 were waited for; matrix products, arithmetic and copies ran while one was open for 5% of the time, Pallas kernels for 0%

commit v1 on v0

v1 whole, which is shorter than its diff:
```python
import jax
import jax.numpy as jnp
from jax import lax
from jax.experimental import pallas as pl
from jax.experimental.pallas import tpu as pltpu
from jax.sharding import PartitionSpec as P

MESH = pl.DeviceIdType.MESH
VIEWS = 8
BLOCKS = 2
ZB = 8
TAPS = 65
REACH = 48
TILE = 128
COLS = 2048
SPAN = TILE + 2 * REACH
PADDED = COLS + 128
UNIT = 16
ORDER = (0, 1, 2, 5, 6, 7, 3, 4)
CHUNKS = len(ORDER)
GROUPS = CHUNKS // 2
STEPS = (1, 3, 2)


def split(value):
    high = value.astype(jnp.bfloat16)
    low = (value - high.astype(jnp.float32)).astype(jnp.bfloat16)
    return high, low


def dot(a, b):
    return jnp.dot(a, b, preferred_element_type=jnp.float32)


def kernel(
    est_ref, views_ref, taps_ref, out_ref,
    arr, image, est, est_hi, est_lo, win_hi, win_lo, bwin_hi, bwin_lo,
    spread_hi, spread_lo, acc, edges, band_x, band_xt, band_f, band_b, rows_x,
    x_sem, y_sem, r_sem, e_sem, es_sem, c_sem, cs_sem, l_sem,
):
    tile = lax.axis_index("joined")
    position = lax.axis_index("view")
    y = position // 4
    x = position % 4
    tiles = 8
    up = lax.rem(tile + 1, tiles)
    down = lax.rem(tile + tiles - 1, tiles)

    barrier = pltpu.get_barrier_semaphore()
    peers = [(tile, y * 4 + (x + d) % 4) for d in (1, 2, 3)]
    peers += [(tile, ((y + d) % 4) * 4 + x) for d in (1, 2, 3)]
    peers += [(up, position), (down, position)]
    for peer in peers:
        pl.semaphore_signal(barrier, inc=1, device_id=peer, device_id_type=MESH)
    pl.semaphore_wait(barrier, len(peers))

    def halo(side):
        if side == 0:
            return pltpu.make_async_remote_copy(
                est_ref.at[0, pl.ds(TILE - REACH, REACH)], est.at[pl.ds(0, REACH)],
                es_sem.at[0], e_sem.at[0], device_id=(up, position), device_id_type=MESH)
        return pltpu.make_async_remote_copy(
            est_ref.at[0, pl.ds(0, REACH)], est.at[pl.ds(REACH + TILE, REACH)],
            es_sem.at[1], e_sem.at[1], device_id=(down, position), device_id_type=MESH)

    halo(0).start()
    halo(1).start()
    own_est = pltpu.make_async_copy(est_ref.at[0], est.at[pl.ds(REACH, TILE)], l_sem)
    own_est.start()

    def side_of(turn):
        return (turn + y + 1) % 2

    def x_copy(index, turn, c):
        rows = pl.ds(ORDER[c] * UNIT, UNIT)
        h = side_of(turn)
        x2 = (x + STEPS[index]) % 4
        y2 = BLOCKS * (x % 2) + h
        slot = jnp.where(y2 == y, 2 * y + x // 2, VIEWS + 2 * x + h)
        return pltpu.make_async_remote_copy(
            views_ref.at[0, 4 * h + x2, rows], arr.at[slot, rows],
            x_sem.at[index, turn, c], r_sem.at[slot, c],
            device_id=(tile, y * 4 + x2), device_id_type=MESH)

    def y_copy(step, turn, c):
        rows = pl.ds(ORDER[c] * UNIT, UNIT)
        h = side_of(turn)
        xs = (x - step) % 4
        y2 = BLOCKS * (xs % 2) + h
        k = 2 * y + xs // 2
        slot = VIEWS + 2 * xs + h
        source = views_ref.at[0, 4 * h + x, rows] if step == 0 else arr.at[slot, rows]
        remote = pltpu.make_async_remote_copy(
            source, arr.at[k, rows], y_sem.at[step, turn, c], r_sem.at[k, c],
            device_id=(tile, y2 * 4 + x), device_id_type=MESH)
        local = pltpu.make_async_copy(source, arr.at[k, rows], r_sem.at[k, c])
        return y2 != y, slot, remote, local

    def arrived(slot, c):
        rows = pl.ds(ORDER[c] * UNIT, UNIT)
        pltpu.make_async_copy(
            views_ref.at[0, 0, rows], arr.at[slot, rows], r_sem.at[slot, c]).wait()

    for c in range(CHUNKS):
        for index in range(3):
            for turn in range(2):
                x_copy(index, turn, c).start()
    for c in range(CHUNKS):
        for turn in range(2):
            away, _, remote, local = y_copy(0, turn, c)

            @pl.when(away)
            def _():
                remote.start()

            @pl.when(jnp.logical_not(away))
            def _():
                local.start()

    def relay(c):
        for turn in range(2):
            for step in STEPS:
                away, slot, remote, _ = y_copy(step, turn, c)

                @pl.when(away)
                def _():
                    arrived(slot, c)
                    remote.start()

    @pl.loop(0, VIEWS)
    def _(k):
        row = jnp.broadcast_to(taps_ref[pl.ds(k, 1), :], (TILE, 256))
        band = pltpu.roll(row, 0, 1, stride=1, stride_axis=0)
        rows_x[k] = band
        high, low = split(band)
        band_x[k, 0:TILE, :] = high
        band_x[k, TILE : 2 * TILE, :] = low
        for first, target in ((VIEWS, band_f), (2 * VIEWS, band_b)):
            row = jnp.broadcast_to(taps_ref[pl.ds(first + k, 1), :], (256, 256))
            band = pltpu.roll(row, 0, 1, stride=1, stride_axis=0)[:, :128]
            high, low = split(band)
            target[k, :, 0:128] = high
            target[k, :, 128:256] = low

    for g in range(GROUPS):
        first, second = ORDER[2 * g] * UNIT, ORDER[2 * g + 1] * UNIT
        picked = jnp.concatenate(
            [rows_x[:, first : first + UNIT, :], rows_x[:, second : second + UNIT, :]], axis=1)
        band = jnp.transpose(picked.reshape(256, 256))
        high, low = split(band)
        band_xt[g, 0:256, :] = high
        band_xt[g, 256:512, :] = low

    own_est.wait()
    halo(0).wait_recv()
    halo(1).wait_recv()
    est[SPAN:256, :] = jnp.zeros((256 - SPAN, COLS), jnp.float32)

    @pl.loop(0, 256 // 32)
    def _(i):
        rows = pl.ds(pl.multiple_of(i * 32, 32), 32)
        high, low = split(pltpu.roll(est[rows, :], 64, 1))
        est_hi[rows, 0:COLS] = high
        est_lo[rows, 0:COLS] = low
        est_hi[rows, COLS:PADDED] = high[:, 0:128]
        est_lo[rows, COLS:PADDED] = low[:, 0:128]

    @pl.loop(0, VIEWS)
    def _(k):
        for first in range(0, PADDED, 256):
            width = min(256, PADDED - first)
            cols = pl.ds(first, width)
            wide = dot(band_x[k], est_hi[:, cols])
            value = wide[:TILE] + wide[TILE:] + dot(band_x[k, 0:TILE, :], est_lo[:, cols])
            high, low = split(value)
            for part in range(width // 128):
                b = first // 128 + part
                piece = slice(128 * part, 128 * part + 128)
                if b < 16:
                    win_hi[b, :, 0:128] = high[:, piece]
                    win_lo[b, :, 0:128] = low[:, piece]
                if b > 0:
                    win_hi[b - 1, :, 128:256] = high[:, piece]
                    win_lo[b - 1, :, 128:256] = low[:, piece]
        for b in range(0, 16, 4):
            wide = dot(win_hi[b : b + 4].reshape(512, 256), band_f[k])
            value = wide[:, :128] + wide[:, 128:]
            value = value + dot(win_lo[b : b + 4].reshape(512, 256), band_f[k, :, 0:128])
            for part in range(4):
                image[k, :, 128 * (b + part) : 128 * (b + part) + 128] = value[
                    128 * part : 128 * part + 128]

    def backward(g):
        first, second = ORDER[2 * g] * UNIT, ORDER[2 * g + 1] * UNIT

        @pl.loop(0, VIEWS)
        def _(k):
            arrived(k, 2 * g)
            arrived(k, 2 * g + 1)
            for half, start in ((0, first), (1, second)):
                rows = slice(start, start + UNIT)
                ratio = arr[k, rows, :] / image[k, rows, :]
                high, low = split(pltpu.roll(ratio, 64, 1))
                into = slice(half * UNIT, half * UNIT + UNIT)
                for b in range(16):
                    piece = slice(128 * b, 128 * b + 128)
                    before = (b - 1) % 16
                    bwin_hi[b, into, 0:128] = high[:, piece]
                    bwin_lo[b, into, 0:128] = low[:, piece]
                    bwin_hi[before, into, 128:256] = high[:, piece]
                    bwin_lo[before, into, 128:256] = low[:, piece]
            wide = dot(bwin_hi[...].reshape(512, 256), band_b[k])
            value = wide[:, :128] + wide[:, 128:]
            value = value + dot(bwin_lo[...].reshape(512, 256), band_b[k, :, 0:128])
            high, low = split(value)
            for b in range(16):
                spread_hi[k, :, 128 * b : 128 * b + 128] = high[32 * b : 32 * b + 32]
                spread_lo[k, :, 128 * b : 128 * b + 128] = low[32 * b : 32 * b + 32]

        inner = g == GROUPS - 1
        base, count = (REACH, TILE) if inner else (0, 256)
        for start in range(0, COLS, 256):
            cols = slice(start, start + 256)
            high = spread_hi[:, :, cols].reshape(256, 256)
            low = spread_lo[:, :, cols].reshape(256, 256)
            value = dot(band_xt[g, base : base + count, :], high)
            value = value + dot(band_xt[g, 256 + base : 256 + base + count, :], high)
            value = value + dot(band_xt[g, base : base + count, :], low)
            if g == 0:
                acc[:, cols] = value
            else:
                acc[base : base + count, cols] += value

    def edge(side):
        if side == 0:
            return pltpu.make_async_remote_copy(
                acc.at[pl.ds(REACH + TILE, REACH)], edges.at[0],
                cs_sem.at[0], c_sem.at[0], device_id=(up, position), device_id_type=MESH)
        return pltpu.make_async_remote_copy(
            acc.at[pl.ds(0, REACH)], edges.at[1],
            cs_sem.at[1], c_sem.at[1], device_id=(down, position), device_id_type=MESH)

    relay(0)
    relay(1)
    relay(2)
    backward(0)
    relay(3)
    relay(4)
    backward(1)
    relay(5)
    relay(6)
    backward(2)
    relay(7)
    edge(0).start()
    edge(1).start()
    backward(3)
    edge(0).wait_recv()
    edge(1).wait_recv()
    count = jnp.broadcast_to(taps_ref[3 * VIEWS : 3 * VIEWS + 1, 0:128], (UNIT, 128))
    for part in range(TILE // UNIT):
        rows = slice(REACH + part * UNIT, REACH + part * UNIT + UNIT)
        total = acc[rows, :]
        if part < REACH // UNIT:
            total = total + edges[0, part * UNIT : part * UNIT + UNIT, :]
        if part >= (TILE - REACH) // UNIT:
            low_row = part * UNIT - (TILE - REACH)
            total = total + edges[1, low_row : low_row + UNIT, :]
        value = est[rows, :] * total
        for b in range(16):
            cols = slice(128 * b, 128 * b + 128)
            out_ref[0, part * UNIT : part * UNIT + UNIT, cols] = value[:, cols] / count

    halo(0).wait_send()
    halo(1).wait_send()
    edge(0).wait_send()
    edge(1).wait_send()
    for c in range(CHUNKS):
        for turn in range(2):
            for index in range(3):
                x_copy(index, turn, c).wait_send()
            for step in range(4):
                away, _, remote, _ = y_copy(step, turn, c)

                @pl.when(away)
                def _():
                    remote.wait_send()


def prepare(psf, offsets, lengths):
    position = lax.axis_index("view")
    block, row = position // ZB, position % ZB
    kernels = psf / jnp.sum(psf, axis=2, keepdims=True)
    block_lengths = lax.dynamic_index_in_dim(lengths, block, 1, keepdims=False)
    live = (row < block_lengths).astype(jnp.float32)
    lane = jnp.arange(256, dtype=jnp.int32)[None, :]
    tap = jnp.arange(TAPS, dtype=jnp.int32)
    dx, dy = offsets[:, 0:1], offsets[:, 1:2]

    def place(index, taps):
        onehot = index[:, :, None] == tap[None, None, :]
        return jnp.sum(jnp.where(onehot, taps[:, None, :], 0.0), axis=2)

    rows = [
        place(lane - 16 - dx, kernels[:, 0]),
        place(224 - lane - dy, kernels[:, 1]),
        place(lane - 160 - dy, kernels[:, 1] * live[:, None]),
        jnp.full((VIEWS, 256), jnp.sum(live), jnp.float32),
    ]
    return jnp.concatenate(rows, axis=0)


def per_device(estimate, views, psf, offsets, lengths):
    taps = prepare(psf, offsets, lengths)
    f32, bf16 = jnp.float32, jnp.bfloat16
    anywhere = pl.BlockSpec(memory_space=pl.ANY)
    vmem = pl.BlockSpec(memory_space=pltpu.VMEM)
    dma = pltpu.SemaphoreType.DMA
    return pl.pallas_call(
        kernel,
        out_shape=jax.ShapeDtypeStruct(estimate.shape, f32),
        in_specs=[anywhere, anywhere, vmem],
        out_specs=vmem,
        scratch_shapes=[
            pltpu.VMEM((2 * VIEWS, TILE, COLS), f32),
            pltpu.VMEM((VIEWS, TILE, COLS), f32),
            pltpu.VMEM((256, COLS), f32),
            pltpu.VMEM((256, PADDED), bf16),
            pltpu.VMEM((256, PADDED), bf16),
            pltpu.VMEM((16, TILE, 256), bf16),
            pltpu.VMEM((16, TILE, 256), bf16),
            pltpu.VMEM((16, 2 * UNIT, 256), bf16),
            pltpu.VMEM((16, 2 * UNIT, 256), bf16),
            pltpu.VMEM((VIEWS, 2 * UNIT, COLS), bf16),
            pltpu.VMEM((VIEWS, 2 * UNIT, COLS), bf16),
            pltpu.VMEM((256, COLS), f32),
            pltpu.VMEM((2, REACH, COLS), f32),
            pltpu.VMEM((VIEWS, 2 * TILE, 256), bf16),
            pltpu.VMEM((GROUPS, 512, 256), bf16),
            pltpu.VMEM((VIEWS, 256, 256), bf16),
            pltpu.VMEM((VIEWS, 256, 256), bf16),
            pltpu.VMEM((VIEWS, TILE, 256), f32),
            dma((3, 2, CHUNKS)),
            dma((4, 2, CHUNKS)),
            dma((2 * VIEWS, CHUNKS)),
            dma((2,)),
            dma((2,)),
            dma((2,)),
            dma((2,)),
            dma,
        ],
        compiler_params=pltpu.CompilerParams(
            collective_id=0, has_side_effects=True, vmem_limit_bytes=60 * 2**20
        ),
        name="deconvolve",
    )(estimate, views, taps)


def solution(mesh):
    return jax.shard_map(
        per_device,
        mesh=mesh,
        in_specs=(P("view", "joined", None), P("view", None, "joined", None), P(), P(), P()),
        out_specs=P("view", "joined", None),
        check_vma=False,
    )
```

time: 546 us -> 147 us (0.27); the launches traced: 537 us -> 145 us
  waiting for transfers between devices: 265 us -> 0 us
  local copies, waits for them, and re-layouts: 145 us -> 4.07 us
  Pallas kernels: 0 us -> 136 us
  matrix products: 71.7 us -> 0 us
  other arithmetic: 30.8 us -> 4.79 us
  between operations: 18.1 us -> 0.04 us
  starting transfers between devices: 5.95 us -> 0 us
    pallas_call x0 -> x1, Pallas kernels: none -> 136 us  [per_device(): pl.pallas_call(kernel, out_shape=jax.ShapeDtypeStruct(estimate.shape, f32...]
    all_gather x1 -> x0, waiting for transfers between devices: 115 us -> none  [per_device(): whole = lax.all_gather(current, 'view', axis=0, tiled=True)]
    unnamed x3 -> x0, waiting for transfers between devices: 110 us -> none
    dot_general x8 -> x0, matrix products: 71.7 us -> none  [the longest x2 27.5 us: blur_lateral(): jnp.einsum('zxje,et->zxjt', stacked, band, precision=lax.Precision.HIGHEST)]
    slice x11 -> x1, local copies, waits for them, and re-layouts: 46.8 us -> 0.76 us  [prepare(): dx, dy = (offsets[:, 0:1], offsets[:, 1:2])]
    ppermute x4 -> x0, waiting for transfers between devices: 40.2 us -> none  [the longest x2 40.2 us: padded_2(): before = lax.ppermute(last, axis, up)]
    concatenate x4 -> x1, local copies, waits for them, and re-layouts: 30.6 us -> 0.07 us  [prepare(): return jnp.concatenate(rows, axis=0)]
    reshape x3 -> x0, local copies, waits for them, and re-layouts: 28.2 us -> none  [the longest x2 18.9 us: blur_lateral(): window[:, :, :lateral_cols]]
  transfers between devices with their start and end apart: 6 -> 0, of which waited for: 4 -> 0; matrix products, arithmetic and copies ran while one was open for 5% -> 0% of each run, Pallas kernels for 0% -> 0%
where the time goes in v1:
time: 147 us; the launch traced here: 145 us
  Pallas kernels  136 us (93%)
  other arithmetic  4.79 us (3%)
  local copies, waits for them, and re-layouts  4.07 us (3%)
    pallas_call x1, Pallas kernels, per_device(): pl.pallas_call(kernel, out_shape=jax.ShapeDtypeStruct(estimate.shape, f32...  136 us

profile of v1, /device:TPU:24, one launch (start us, length us, event | category | flops | bytes accessed | tf_op | source)
XLA Modules:
  0.0 145.2 jit_solution(13431636476584138914)
XLA Ops:
  0.0 1.3 fusion
  1.3 0.7 fusion.1
  2.0 0.6 broadcast_in_dim.50
  2.6 0.1 pad.3.clone
  2.7 0.8 slice_bitcast_fusion.1
  3.5 0.8 reduce_sum.45
  4.3 0.8 broadcast_divide_fusion
  5.0 0.1 fusion.2
  5.1 0.1 broadcast_subtract_fusion.1
  5.2 0.1 copy.8
  5.3 0.1 select_reduce_fusion
  5.4 0.1 copy.6
  5.5 0.1 select_reduce_fusion.2
  5.7 0.1 copy.7
  5.8 0.1 select_reduce_fusion.1
  5.9 0.7 maximum_maximum_fusion.taps_ref
  6.6 136.3 %deconvolve.1 = f32[1,128,2048]{2,1,0:T(8,128)} custom-call(f32[1,128,2048]{2,1,0:T(8,128)} %est_ref.1, f32[1,8,128,2048]{3,2,1,0:T(8,128)} %views_ref.1, f32[32,256]{1,0:T(8,128)} %maximum_maximum_fusion.taps_ref), custom_call_target="tpu_custom_call" | custom-call | tf_op jit(solution)/shard_map/deconvolve/pallas_call | solution.py:318
  142.9 2.3 %copy.10 = f32[1,128,2048]{2,1,0:T(8,128)} copy(f32[1,128,2048]{2,1,0:T(8,128)} %deconvolve.1) | data formatting | bytes 2097152
  (3 shorter events, 0.0 us)

commit v2 on v1

--- a/solution.py
+++ b/solution.py
@@ -20,6 +20,45 @@
 CHUNKS = len(ORDER)
 GROUPS = CHUNKS // 2
 STEPS = (1, 3, 2)
+AHEAD = 3
+LAG = 1
+SKEW = 1
+
+
+def travel():
+    turns = []
+    for t in range(CHUNKS + SKEW):
+        if t < CHUNKS:
+            turns.append((t, (1, 3)))
+        if t >= SKEW:
+            turns.append((t - SKEW, (2,)))
+    return turns
+
+
+def plan():
+    items, done = [], 0
+    for index, (c, steps) in enumerate(TRAVEL):
+        if index == 0:
+            items.append(("forward", 0, 4))
+        items.append(("relay", c, steps))
+        if 1 in steps and c + AHEAD < CHUNKS:
+            items.append(("own", c + AHEAD))
+        if index == 1:
+            items.append(("forward", 4, VIEWS))
+        if 2 in steps:
+            ready = c - LAG if c < CHUNKS - 1 else CHUNKS - 1
+            while done <= ready:
+                if done == CHUNKS - 2:
+                    items.append(("edge",))
+                items.append(("y", done))
+                if done % 2:
+                    items.append(("x", done // 2))
+                done += 1
+    return items
+
+
+TRAVEL = travel()
+PLAN = plan()
 
 
 def split(value):
@@ -33,9 +72,9 @@
 
 
 def kernel(
-    est_ref, views_ref, taps_ref, out_ref,
+    est_ref, views_ref, psf_ref, offsets_ref, lengths_ref, out_ref,
     arr, image, est, est_hi, est_lo, win_hi, win_lo, bwin_hi, bwin_lo,
-    spread_hi, spread_lo, acc, edges, band_x, band_xt, band_f, band_b, rows_x,
+    spread_hi, spread_lo, acc, edges, band_x, band_xt, band_f, band_b, rows_x, taps_ref,
     x_sem, y_sem, r_sem, e_sem, es_sem, c_sem, cs_sem, l_sem,
 ):
     tile = lax.axis_index("joined")
@@ -82,50 +121,77 @@
             x_sem.at[index, turn, c], r_sem.at[slot, c],
             device_id=(tile, y * 4 + x2), device_id_type=MESH)
 
-    def y_copy(step, turn, c):
-        rows = pl.ds(ORDER[c] * UNIT, UNIT)
+    def y_route(step, turn, c):
         h = side_of(turn)
         xs = (x - step) % 4
         y2 = BLOCKS * (xs % 2) + h
-        k = 2 * y + xs // 2
-        slot = VIEWS + 2 * xs + h
-        source = views_ref.at[0, 4 * h + x, rows] if step == 0 else arr.at[slot, rows]
-        remote = pltpu.make_async_remote_copy(
+        return pl.ds(ORDER[c] * UNIT, UNIT), h, xs, y2, 2 * y + xs // 2
+
+    def y_copy(step, turn, c):
+        rows, h, xs, y2, k = y_route(step, turn, c)
+        source = views_ref.at[0, 4 * h + x, rows] if step == 0 else arr.at[VIEWS + 2 * xs + h, rows]
+        return pltpu.make_async_remote_copy(
             source, arr.at[k, rows], y_sem.at[step, turn, c], r_sem.at[k, c],
             device_id=(tile, y2 * 4 + x), device_id_type=MESH)
-        local = pltpu.make_async_copy(source, arr.at[k, rows], r_sem.at[k, c])
-        return y2 != y, slot, remote, local
 
     def arrived(slot, c):
         rows = pl.ds(ORDER[c] * UNIT, UNIT)
         pltpu.make_async_copy(
             views_ref.at[0, 0, rows], arr.at[slot, rows], r_sem.at[slot, c]).wait()
 
-    for c in range(CHUNKS):
-        for index in range(3):
-            for turn in range(2):
-                x_copy(index, turn, c).start()
-    for c in range(CHUNKS):
+    def own(c):
         for turn in range(2):
-            away, _, remote, local = y_copy(0, turn, c)
-
-            @pl.when(away)
+            rows, h, _, y2, k = y_route(0, turn, c)
+
+            @pl.when(y2 != y)
             def _():
-                remote.start()
-
-            @pl.when(jnp.logical_not(away))
+                y_copy(0, turn, c).start()
+
+            @pl.when(y2 == y)
             def _():
-                local.start()
-
-    def relay(c):
+                pltpu.make_async_copy(
+                    views_ref.at[0, 4 * h + x, rows], arr.at[k, rows], r_sem.at[k, c]).start()
+
+    def relay(c, steps):
         for turn in range(2):
-            for step in STEPS:
-                away, slot, remote, _ = y_copy(step, turn, c)
-
-                @pl.when(away)
+            for step in steps:
+                _, h, xs, y2, _ = y_route(step, turn, c)
+
+                @pl.when(y2 != y)
                 def _():
-                    arrived(slot, c)
-                    remote.start()
+                    arrived(VIEWS + 2 * xs + h, c)
+                    y_copy(step, turn, c).start()
+
+    for c, steps in TRAVEL:
+        for index, step in enumerate(STEPS):
+            if step in steps:
+                for turn in range(2):
+                    x_copy(index, turn, c).start()
+    for c in range(AHEAD):
+        own(c)
+
+    block, plane_row = position // ZB, position % ZB
+    blank = jnp.zeros((VIEWS, 128 - TAPS), jnp.float32)
+    columns = []
+    for axis in range(2):
+        taps = psf_ref[:, axis, :]
+        taps = taps / jnp.sum(taps, axis=1, keepdims=True)
+        columns.append(jnp.transpose(jnp.concatenate([taps, blank], axis=1)))
+    tap = lax.broadcasted_iota(jnp.int32, (128, 256), 0)
+    lane = lax.broadcasted_iota(jnp.int32, (128, 256), 1)
+    total = jnp.zeros((VIEWS, 256), jnp.float32)
+    for k in range(VIEWS):
+        live = jnp.where(plane_row < lengths_ref[k, block], 1.0, 0.0)
+        total = total + live
+        dx, dy = offsets_ref[k, 0], offsets_ref[k, 1]
+        places = ((0, lane - 16 - dx), (1, 224 - lane - dy), (1, lane - 160 - dy))
+        for kind, (axis, place) in enumerate(places):
+            column = jnp.broadcast_to(columns[axis][:, k : k + 1], (128, 256))
+            line = jnp.sum(jnp.where(place == tap, column, 0.0), axis=0, keepdims=True)
+            if kind == 2:
+                line = line * live
+            taps_ref[kind * VIEWS + k : kind * VIEWS + k + 1, :] = line
+    taps_ref[3 * VIEWS : 4 * VIEWS, :] = total
 
     @pl.loop(0, VIEWS)
     def _(k):
@@ -165,8 +231,7 @@
         est_hi[rows, COLS:PADDED] = high[:, 0:128]
         est_lo[rows, COLS:PADDED] = low[:, 0:128]
 
-    @pl.loop(0, VIEWS)
-    def _(k):
+    def forward(k):
         for first in range(0, PADDED, 256):
             width = min(256, PADDED - first)
             cols = pl.ds(first, width)
@@ -190,33 +255,32 @@
                 image[k, :, 128 * (b + part) : 128 * (b + part) + 128] = value[
                     128 * part : 128 * part + 128]
 
-    def backward(g):
-        first, second = ORDER[2 * g] * UNIT, ORDER[2 * g + 1] * UNIT
+    def back_y(c):
+        start = ORDER[c] * UNIT
 
         @pl.loop(0, VIEWS)
         def _(k):
-            arrived(k, 2 * g)
-            arrived(k, 2 * g + 1)
-            for half, start in ((0, first), (1, second)):
-                rows = slice(start, start + UNIT)
-                ratio = arr[k, rows, :] / image[k, rows, :]
-                high, low = split(pltpu.roll(ratio, 64, 1))
-                into = slice(half * UNIT, half * UNIT + UNIT)
-                for b in range(16):
-                    piece = slice(128 * b, 128 * b + 128)
-                    before = (b - 1) % 16
-                    bwin_hi[b, into, 0:128] = high[:, piece]
-                    bwin_lo[b, into, 0:128] = low[:, piece]
-                    bwin_hi[before, into, 128:256] = high[:, piece]
-                    bwin_lo[before, into, 128:256] = low[:, piece]
-            wide = dot(bwin_hi[...].reshape(512, 256), band_b[k])
+            arrived(k, c)
+            rows = slice(start, start + UNIT)
+            ratio = arr[k, rows, :] / image[k, rows, :]
+            high, low = split(pltpu.roll(ratio, 64, 1))
+            for b in range(16):
+                piece = slice(128 * b, 128 * b + 128)
+                before = (b - 1) % 16
+                bwin_hi[b, :, 0:128] = high[:, piece]
+                bwin_lo[b, :, 0:128] = low[:, piece]
+                bwin_hi[before, :, 128:256] = high[:, piece]
+                bwin_lo[before, :, 128:256] = low[:, piece]
+            wide = dot(bwin_hi[...].reshape(256, 256), band_b[k])
             value = wide[:, :128] + wide[:, 128:]
-            value = value + dot(bwin_lo[...].reshape(512, 256), band_b[k, :, 0:128])
+            value = value + dot(bwin_lo[...].reshape(256, 256), band_b[k, :, 0:128])
             high, low = split(value)
+            into = slice((c % 2) * UNIT, (c % 2) * UNIT + UNIT)
             for b in range(16):
-                spread_hi[k, :, 128 * b : 128 * b + 128] = high[32 * b : 32 * b + 32]
-                spread_lo[k, :, 128 * b : 128 * b + 128] = low[32 * b : 32 * b + 32]
-
+                spread_hi[k, into, 128 * b : 128 * b + 128] = high[16 * b : 16 * b + 16]
+                spread_lo[k, into, 128 * b : 128 * b + 128] = low[16 * b : 16 * b + 16]
+
+    def back_x(g):
         inner = g == GROUPS - 1
         base, count = (REACH, TILE) if inner else (0, 256)
         for start in range(0, COLS, 256):
@@ -240,20 +304,20 @@
             acc.at[pl.ds(0, REACH)], edges.at[1],
             cs_sem.at[1], c_sem.at[1], device_id=(down, position), device_id_type=MESH)
 
-    relay(0)
-    relay(1)
-    relay(2)
-    backward(0)
-    relay(3)
-    relay(4)
-    backward(1)
-    relay(5)
-    relay(6)
-    backward(2)
-    relay(7)
-    edge(0).start()
-    edge(1).start()
-    backward(3)
+    for item in PLAN:
+        if item[0] == "own":
+            own(item[1])
+        elif item[0] == "relay":
+            relay(item[1], item[2])
+        elif item[0] == "y":
+            back_y(item[1])
+        elif item[0] == "x":
+            back_x(item[1])
+        elif item[0] == "edge":
+            edge(0).start()
+            edge(1).start()
+        else:
+            pl.loop(item[1], item[2])(forward)
     edge(0).wait_recv()
     edge(1).wait_recv()
     count = jnp.broadcast_to(taps_ref[3 * VIEWS : 3 * VIEWS + 1, 0:128], (UNIT, 128))
@@ -279,46 +343,23 @@
             for index in range(3):
                 x_copy(index, turn, c).wait_send()
             for step in range(4):
-                away, _, remote, _ = y_copy(step, turn, c)
-
-                @pl.when(away)
+                _, _, _, y2, _ = y_route(step, turn, c)
+
+                @pl.when(y2 != y)
                 def _():
-                    remote.wait_send()
-
-
-def prepare(psf, offsets, lengths):
-    position = lax.axis_index("view")
-    block, row = position // ZB, position % ZB
-    kernels = psf / jnp.sum(psf, axis=2, keepdims=True)
-    block_lengths = lax.dynamic_index_in_dim(lengths, block, 1, keepdims=False)
-    live = (row < block_lengths).astype(jnp.float32)
-    lane = jnp.arange(256, dtype=jnp.int32)[None, :]
-    tap = jnp.arange(TAPS, dtype=jnp.int32)
-    dx, dy = offsets[:, 0:1], offsets[:, 1:2]
-
-    def place(index, taps):
-        onehot = index[:, :, None] == tap[None, None, :]
-        return jnp.sum(jnp.where(onehot, taps[:, None, :], 0.0), axis=2)
-
-    rows = [
-        place(lane - 16 - dx, kernels[:, 0]),
-        place(224 - lane - dy, kernels[:, 1]),
-        place(lane - 160 - dy, kernels[:, 1] * live[:, None]),
-        jnp.full((VIEWS, 256), jnp.sum(live), jnp.float32),
-    ]
-    return jnp.concatenate(rows, axis=0)
+                    y_copy(step, turn, c).wait_send()
 
 
 def per_device(estimate, views, psf, offsets, lengths):
-    taps = prepare(psf, offsets, lengths)
     f32, bf16 = jnp.float32, jnp.bfloat16
     anywhere = pl.BlockSpec(memory_space=pl.ANY)
     vmem = pl.BlockSpec(memory_space=pltpu.VMEM)
+    smem = pl.BlockSpec(memory_space=pltpu.SMEM)
     dma = pltpu.SemaphoreType.DMA
     return pl.pallas_call(
         kernel,
         out_shape=jax.ShapeDtypeStruct(estimate.shape, f32),
-        in_specs=[anywhere, anywhere, vmem],
+        in_specs=[anywhere, anywhere, vmem, smem, smem],
         out_specs=vmem,
         scratch_shapes=[
             pltpu.VMEM((2 * VIEWS, TILE, COLS), f32),
@@ -328,8 +369,8 @@
             pltpu.VMEM((256, PADDED), bf16),
             pltpu.VMEM((16, TILE, 256), bf16),
             pltpu.VMEM((16, TILE, 256), bf16),
-            pltpu.VMEM((16, 2 * UNIT, 256), bf16),
-            pltpu.VMEM((16, 2 * UNIT, 256), bf16),
+            pltpu.VMEM((16, UNIT, 256), bf16),
+            pltpu.VMEM((16, UNIT, 256), bf16),
             pltpu.VMEM((VIEWS, 2 * UNIT, COLS), bf16),
             pltpu.VMEM((VIEWS, 2 * UNIT, COLS), bf16),
             pltpu.VMEM((256, COLS), f32),
@@ -339,6 +380,7 @@
             pltpu.VMEM((VIEWS, 256, 256), bf16),
             pltpu.VMEM((VIEWS, 256, 256), bf16),
             pltpu.VMEM((VIEWS, TILE, 256), f32),
+            pltpu.VMEM((4 * VIEWS, 256), f32),
             dma((3, 2, CHUNKS)),
             dma((4, 2, CHUNKS)),
             dma((2 * VIEWS, CHUNKS)),
@@ -352,7 +394,7 @@
             collective_id=0, has_side_effects=True, vmem_limit_bytes=60 * 2**20
         ),
         name="deconvolve",
-    )(estimate, views, taps)
+    )(estimate, views, psf, offsets, lengths)
 
 
 def solution(mesh):

time: 147 us -> 121 us (0.82); the launches traced: 145 us -> 121 us
  Pallas kernels: 136 us -> 116 us
  other arithmetic: 4.79 us -> 0 us
    pallas_call x1, Pallas kernels: 136 us -> 116 us  [per_device(): pl.pallas_call(kernel, out_shape=jax.ShapeDtypeStruct(estimate.shape, f32...]
    unnamed x1 -> x3, local copies, waits for them, and re-layouts: 2.3 us -> 4.98 us
    reduce_sum x5 -> x0, other arithmetic: 2.47 us -> none  [the longest x1 1.29 us: prepare(): jnp.sum(live)]
where the time goes in v2:
time: 121 us
  Pallas kernels  116 us (96%)
  local copies, waits for them, and re-layouts  4.98 us (4%)
    pallas_call x1, Pallas kernels, per_device(): pl.pallas_call(kernel, out_shape=jax.ShapeDtypeStruct(estimate.shape, f32...  116 us
    unnamed x3, local copies, waits for them, and re-layouts  4.98 us

profile of v2, /device:TPU:24, one launch (start us, length us, event | category | flops | bytes accessed | tf_op | source)
XLA Modules:
  0.0 120.8 jit_solution(2440057641313864704)
XLA Ops:
  0.0 1.3 %copy.6.offsets_ref = s32[8,2]{1,0:T(8,128)} copy(s32[8,2]{0,1:T(2,128)} %param.8) | data formatting | bytes 128 | tf_op args[3]
  1.3 1.3 %copy.7.lengths_ref = s32[8,2]{1,0:T(8,128)} copy(s32[8,2]{0,1:T(2,128)} %param.9) | data formatting | bytes 128 | tf_op args[4]
  2.7 115.8 %deconvolve.1 = f32[1,128,2048]{2,1,0:T(8,128)} custom-call(f32[1,128,2048]{2,1,0:T(8,128)} %est_ref.1, f32[1,8,128,2048]{3,2,1,0:T(8,128)} %views_ref.1, f32[8,2,65]{2,1,0:T(2,128)} %psf_ref.1, s32[8,2]{1,0:T(8,128)} %copy.6.offsets_ref, s32[8,2]{1,0:T(8,128)} %copy.7.lengths_ref), custom_call_target="tpu_custom_call" | custom-call | tf_op jit(solution)/shard_map/deconvolve/pallas_call | solution.py:359
  118.5 2.3 %copy.9 = f32[1,128,2048]{2,1,0:T(8,128)} copy(f32[1,128,2048]{2,1,0:T(8,128)} %deconvolve.1) | data formatting | bytes 2097152

commit v3 on v2

--- a/solution.py
+++ b/solution.py
@@ -21,7 +21,7 @@
 GROUPS = CHUNKS // 2
 STEPS = (1, 3, 2)
 AHEAD = 3
-LAG = 1
+LAG = 2
 SKEW = 1
 
 
@@ -35,26 +35,34 @@
     return turns
 
 
+PACE = 2
+
+
 def plan():
-    items, done = [], 0
-    for index, (c, steps) in enumerate(TRAVEL):
-        if index == 0:
-            items.append(("forward", 0, 4))
-        items.append(("relay", c, steps))
-        if 1 in steps and c + AHEAD < CHUNKS:
-            items.append(("own", c + AHEAD))
-        if index == 1:
-            items.append(("forward", 4, VIEWS))
-        if 2 in steps:
-            ready = c - LAG if c < CHUNKS - 1 else CHUNKS - 1
-            while done <= ready:
-                if done == CHUNKS - 2:
-                    items.append(("edge",))
-                items.append(("y", done))
-                if done % 2:
-                    items.append(("x", done // 2))
-                done += 1
-    return items
+    pieces, last = [], {}
+    for c, steps in TRAVEL:
+        for turn in range(2):
+            for step in steps:
+                pieces.append(("relay", c, step, turn))
+                last[c] = len(pieces) - 1
+    work = [(3, ("estimate",))]
+    work += [(4 + k, ("forward", k)) for k in range(VIEWS)]
+    for c in range(CHUNKS):
+        work += [(last[c] + LAG + near, ("y", c, near)) for near in range(4)]
+        if c % 2:
+            work += [(0, ("x", c // 2, half)) for half in range(2)]
+            if c == CHUNKS - 3:
+                work.append((0, ("edge",)))
+    items = []
+    for index, piece in enumerate(pieces):
+        items.append(piece)
+        c = piece[1] + AHEAD
+        if piece[2:] == (3, 1) and c < CHUNKS:
+            items.append(("own", c))
+        for _ in range(PACE):
+            if work and work[0][0] <= index:
+                items.append(work.pop(0)[1])
+    return items + [item for _, item in work]
 
 
 TRAVEL = travel()
@@ -107,12 +115,13 @@
     own_est = pltpu.make_async_copy(est_ref.at[0], est.at[pl.ds(REACH, TILE)], l_sem)
     own_est.start()
 
-    def side_of(turn):
-        return (turn + y + 1) % 2
+    def side_of(turn, source):
+        home = jnp.where(source % 2 == y // 2, 1, 0)
+        return (turn + y + home) % 2
 
     def x_copy(index, turn, c):
         rows = pl.ds(ORDER[c] * UNIT, UNIT)
-        h = side_of(turn)
+        h = side_of(turn, x)
         x2 = (x + STEPS[index]) % 4
         y2 = BLOCKS * (x % 2) + h
         slot = jnp.where(y2 == y, 2 * y + x // 2, VIEWS + 2 * x + h)
@@ -122,8 +131,8 @@
             device_id=(tile, y * 4 + x2), device_id_type=MESH)
 
     def y_route(step, turn, c):
-        h = side_of(turn)
         xs = (x - step) % 4
+        h = side_of(turn, xs)
         y2 = BLOCKS * (xs % 2) + h
         return pl.ds(ORDER[c] * UNIT, UNIT), h, xs, y2, 2 * y + xs // 2
 
@@ -152,15 +161,13 @@
                 pltpu.make_async_copy(
                     views_ref.at[0, 4 * h + x, rows], arr.at[k, rows], r_sem.at[k, c]).start()
 
-    def relay(c, steps):
-        for turn in range(2):
-            for step in steps:
-                _, h, xs, y2, _ = y_route(step, turn, c)
-
-                @pl.when(y2 != y)
-                def _():
-                    arrived(VIEWS + 2 * xs + h, c)
-                    y_copy(step, turn, c).start()
+    def relay(c, step, turn):
+        _, h, xs, y2, _ = y_route(step, turn, c)
+
+        @pl.when(y2 != y)
+        def _():
+            arrived(VIEWS + 2 * xs + h, c)
+            y_copy(step, turn, c).start()
 
     for c, steps in TRAVEL:
         for index, step in enumerate(STEPS):
@@ -181,9 +188,9 @@
     lane = lax.broadcasted_iota(jnp.int32, (128, 256), 1)
     total = jnp.zeros((VIEWS, 256), jnp.float32)
     for k in range(VIEWS):
-        live = jnp.where(plane_row < lengths_ref[k, block], 1.0, 0.0)
+        live = jnp.where(plane_row < lengths_ref[block, k], 1.0, 0.0)
         total = total + live
-        dx, dy = offsets_ref[k, 0], offsets_ref[k, 1]
+        dx, dy = offsets_ref[0, k], offsets_ref[1, k]
         places = ((0, lane - 16 - dx), (1, 224 - lane - dy), (1, lane - 160 - dy))
         for kind, (axis, place) in enumerate(places):
             column = jnp.broadcast_to(columns[axis][:, k : k + 1], (128, 256))
@@ -214,22 +221,30 @@
             [rows_x[:, first : first + UNIT, :], rows_x[:, second : second + UNIT, :]], axis=1)
         band = jnp.transpose(picked.reshape(256, 256))
         high, low = split(band)
-        band_xt[g, 0:256, :] = high
-        band_xt[g, 256:512, :] = low
-
-    own_est.wait()
-    halo(0).wait_recv()
-    halo(1).wait_recv()
-    est[SPAN:256, :] = jnp.zeros((256 - SPAN, COLS), jnp.float32)
-
-    @pl.loop(0, 256 // 32)
-    def _(i):
-        rows = pl.ds(pl.multiple_of(i * 32, 32), 32)
-        high, low = split(pltpu.roll(est[rows, :], 64, 1))
-        est_hi[rows, 0:COLS] = high
-        est_lo[rows, 0:COLS] = low
-        est_hi[rows, COLS:PADDED] = high[:, 0:128]
-        est_lo[rows, COLS:PADDED] = low[:, 0:128]
+        if g < GROUPS - 1:
+            band_xt[g, 0:256, :] = high
+            band_xt[g, 256:512, :] = low
+        else:
+            band_xt[g, 0:TILE, :] = high[REACH : REACH + TILE]
+            band_xt[g, TILE : 2 * TILE, :] = low[REACH : REACH + TILE]
+
+    def estimate():
+        own_est.wait()
+        halo(0).wait_recv()
+        halo(1).wait_recv()
+        est[SPAN:256, :] = jnp.zeros((256 - SPAN, COLS), jnp.float32)
+
+        @pl.loop(0, 256 // 32)
+        def _(i):
+            rows = pl.ds(pl.multiple_of(i * 32, 32), 32)
+            high, low = split(pltpu.roll(est[rows, :], 64, 1))
+            est_hi[rows, 0:COLS] = high
+            est_lo[rows, 0:COLS] = low
+            est_hi[rows, COLS:PADDED] = high[:, 0:128]
+            est_lo[rows, COLS:PADDED] = low[:, 0:128]
+
+        count = jnp.broadcast_to(taps_ref[3 * VIEWS : 3 * VIEWS + 1, 0:1], (TILE, 1))
+        est[REACH : REACH + TILE, :] = est[REACH : REACH + TILE, :] / count
 
     def forward(k):
         for first in range(0, PADDED, 256):
@@ -255,11 +270,14 @@
                 image[k, :, 128 * (b + part) : 128 * (b + part) + 128] = value[
                     128 * part : 128 * part + 128]
 
-    def back_y(c):
+    def back_y(c, near):
         start = ORDER[c] * UNIT
 
-        @pl.loop(0, VIEWS)
-        def _(k):
+        far = (0, 1, 3, 2)[near]
+
+        @pl.loop(0, 2)
+        def _(turn):
+            k = 2 * ((y + far) % 4) + turn
             arrived(k, c)
             rows = slice(start, start + UNIT)
             ratio = arr[k, rows, :] / image[k, rows, :]
@@ -280,20 +298,29 @@
                 spread_hi[k, into, 128 * b : 128 * b + 128] = high[16 * b : 16 * b + 16]
                 spread_lo[k, into, 128 * b : 128 * b + 128] = low[16 * b : 16 * b + 16]
 
-    def back_x(g):
-        inner = g == GROUPS - 1
-        base, count = (REACH, TILE) if inner else (0, 256)
-        for start in range(0, COLS, 256):
+    def back_x(g, half):
+        for start in range(half * COLS // 2, (half + 1) * COLS // 2, 256):
             cols = slice(start, start + 256)
             high = spread_hi[:, :, cols].reshape(256, 256)
             low = spread_lo[:, :, cols].reshape(256, 256)
-            value = dot(band_xt[g, base : base + count, :], high)
-            value = value + dot(band_xt[g, 256 + base : 256 + base + count, :], high)
-            value = value + dot(band_xt[g, base : base + count, :], low)
+            wide = dot(band_xt[g], high)
+            value = wide[:256] + wide[256:] + dot(band_xt[g, 0:256, :], low)
             if g == 0:
                 acc[:, cols] = value
             else:
-                acc[base : base + count, cols] += value
+                acc[:, cols] += value
+
+    def last_x(half):
+        g = GROUPS - 1
+        for start in range(half * COLS // 2, (half + 1) * COLS // 2, 256):
+            cols = slice(start, start + 256)
+            high = spread_hi[:, :, cols].reshape(256, 256)
+            low = spread_lo[:, :, cols].reshape(256, 256)
+            wide = dot(band_xt[g, 0 : 2 * TILE, :], high)
+            value = wide[:TILE] + wide[TILE:] + dot(band_xt[g, 0:TILE, :], low)
+            value = value + acc[REACH : REACH + TILE, cols]
+            value = value * est[REACH : REACH + TILE, cols]
+            out_ref[0, :, cols] = value
 
     def edge(side):
         if side == 0:
@@ -304,41 +331,7 @@
             acc.at[pl.ds(0, REACH)], edges.at[1],
             cs_sem.at[1], c_sem.at[1], device_id=(down, position), device_id_type=MESH)
 
-    for item in PLAN:
-        if item[0] == "own":
-            own(item[1])
-        elif item[0] == "relay":
-            relay(item[1], item[2])
-        elif item[0] == "y":
-            back_y(item[1])
-        elif item[0] == "x":
-            back_x(item[1])
-        elif item[0] == "edge":
-            edge(0).start()
-            edge(1).start()
-        else:
-            pl.loop(item[1], item[2])(forward)
-    edge(0).wait_recv()
-    edge(1).wait_recv()
-    count = jnp.broadcast_to(taps_ref[3 * VIEWS : 3 * VIEWS + 1, 0:128], (UNIT, 128))
-    for part in range(TILE // UNIT):
-        rows = slice(REACH + part * UNIT, REACH + part * UNIT + UNIT)
-        total = acc[rows, :]
-        if part < REACH // UNIT:
-            total = total + edges[0, part * UNIT : part * UNIT + UNIT, :]
-        if part >= (TILE - REACH) // UNIT:
-            low_row = part * UNIT - (TILE - REACH)
-            total = total + edges[1, low_row : low_row + UNIT, :]
-        value = est[rows, :] * total
-        for b in range(16):
-            cols = slice(128 * b, 128 * b + 128)
-            out_ref[0, part * UNIT : part * UNIT + UNIT, cols] = value[:, cols] / count
-
-    halo(0).wait_send()
-    halo(1).wait_send()
-    edge(0).wait_send()
-    edge(1).wait_send()
-    for c in range(CHUNKS):
+    def sent(c):
         for turn in range(2):
             for index in range(3):
                 x_copy(index, turn, c).wait_send()
@@ -348,6 +341,40 @@
                 @pl.when(y2 != y)
                 def _():
                     y_copy(step, turn, c).wait_send()
+
+    for item in PLAN:
+        if item[0] == "own":
+            own(item[1])
+        elif item[0] == "relay":
+            relay(*item[1:])
+        elif item[0] == "estimate":
+            estimate()
+        elif item[0] == "forward":
+            forward(item[1])
+        elif item[0] == "y":
+            if item[1:] == (CHUNKS - 1, 0):
+                halo(0).wait_send()
+                halo(1).wait_send()
+                for c in range(CHUNKS - 4):
+                    sent(c)
+            if item[1:] == (CHUNKS - 1, 3):
+                edge(0).wait_recv()
+                edge(1).wait_recv()
+                acc[REACH : 2 * REACH, :] += edges[0]
+                acc[TILE : REACH + TILE, :] += edges[1]
+            back_y(*item[1:])
+        elif item[0] == "edge":
+            edge(0).start()
+            edge(1).start()
+        elif item[1] < GROUPS - 1:
+            back_x(*item[1:])
+        else:
+            last_x(item[2])
+
+    edge(0).wait_send()
+    edge(1).wait_send()
+    for c in range(CHUNKS - 4, CHUNKS):
+        sent(c)
 
 
 def per_device(estimate, views, psf, offsets, lengths):
@@ -394,7 +421,7 @@
             collective_id=0, has_side_effects=True, vmem_limit_bytes=60 * 2**20
         ),
         name="deconvolve",
-    )(estimate, views, psf, offsets, lengths)
+    )(estimate, views, psf, offsets.T, lengths.T)
 
 
 def solution(mesh):

time: 121 us -> 112 us (0.926)
  Pallas kernels: 116 us -> 109 us
  local copies, waits for them, and re-layouts: 4.98 us -> 2.3 us
    pallas_call x1, Pallas kernels: 116 us -> 109 us  [per_device(): pl.pallas_call(kernel, out_shape=jax.ShapeDtypeStruct(estimate.shape, f32...]
    unnamed x3 -> x1, local copies, waits for them, and re-layouts: 4.98 us -> 2.3 us
where the time goes in v3:
time: 112 us; the launch traced here: 111 us
  Pallas kernels  109 us (97%)
  local copies, waits for them, and re-layouts  2.3 us (2%)
    pallas_call x1, Pallas kernels, per_device(): pl.pallas_call(kernel, out_shape=jax.ShapeDtypeStruct(estimate.shape, f32...  109 us
    unnamed x1, local copies, waits for them, and re-layouts  2.3 us

profile of v3, /device:TPU:24, one launch (start us, length us, event | category | flops | bytes accessed | tf_op | source)
XLA Modules:
  0.0 110.8 jit_solution(11142107149238632517)
XLA Ops:
  0.0 108.5 %deconvolve.1 = f32[1,128,2048]{2,1,0:T(8,128)} custom-call(f32[1,128,2048]{2,1,0:T(8,128)} %est_ref.1, f32[1,8,128,2048]{3,2,1,0:T(8,128)} %views_ref.1, f32[8,2,65]{2,1,0:T(2,128)} %psf_ref.1, s32[2,8]{1,0:T(2,128)} %bitcast.2, s32[2,8]{1,0:T(2,128)} %bitcast.3), custom_call_target="tpu_custom_call" | custom-call | tf_op jit(solution)/shard_map/deconvolve/pallas_call | solution.py:386
  108.5 2.3 %copy.7 = f32[1,128,2048]{2,1,0:T(8,128)} copy(f32[1,128,2048]{2,1,0:T(8,128)} %deconvolve.1) | data formatting | bytes 2097152

commit v4 on v3

--- a/solution.py
+++ b/solution.py
@@ -21,7 +21,7 @@
 GROUPS = CHUNKS // 2
 STEPS = (1, 3, 2)
 AHEAD = 3
-LAG = 2
+LAG = 3
 SKEW = 1
 
 
@@ -110,10 +110,7 @@
             est_ref.at[0, pl.ds(0, REACH)], est.at[pl.ds(REACH + TILE, REACH)],
             es_sem.at[1], e_sem.at[1], device_id=(down, position), device_id_type=MESH)
 
-    halo(0).start()
-    halo(1).start()
     own_est = pltpu.make_async_copy(est_ref.at[0], est.at[pl.ds(REACH, TILE)], l_sem)
-    own_est.start()
 
     def side_of(turn, source):
         home = jnp.where(source % 2 == y // 2, 1, 0)
@@ -169,13 +166,22 @@
             arrived(VIEWS + 2 * xs + h, c)
             y_copy(step, turn, c).start()
 
-    for c, steps in TRAVEL:
-        for index, step in enumerate(STEPS):
-            if step in steps:
-                for turn in range(2):
-                    x_copy(index, turn, c).start()
-    for c in range(AHEAD):
+    def depart(travel):
+        for c, steps in travel:
+            for turn in range(2):
+                for index, step in enumerate(STEPS):
+                    if step in steps:
+                        x_copy(index, turn, c).start()
+
+    depart(TRAVEL[:1])
+    own(0)
+    halo(0).start()
+    halo(1).start()
+    own_est.start()
+    depart(TRAVEL[1:2])
+    for c in range(1, AHEAD):
         own(c)
+    depart(TRAVEL[2:])
 
     block, plane_row = position // ZB, position % ZB
     blank = jnp.zeros((VIEWS, 128 - TAPS), jnp.float32)
@@ -378,6 +384,7 @@
 
 
 def per_device(estimate, views, psf, offsets, lengths):
+    operands = (estimate, views, psf, offsets.T, lengths.T)
     f32, bf16 = jnp.float32, jnp.bfloat16
     anywhere = pl.BlockSpec(memory_space=pl.ANY)
     vmem = pl.BlockSpec(memory_space=pltpu.VMEM)
@@ -418,10 +425,10 @@
             dma,
         ],
         compiler_params=pltpu.CompilerParams(
-            collective_id=0, has_side_effects=True, vmem_limit_bytes=60 * 2**20
+            collective_id=0, has_side_effects=True, vmem_limit_bytes=50 * 2**20
         ),
         name="deconvolve",
-    )(estimate, views, psf, offsets.T, lengths.T)
+    )(*(pltpu.with_memory_space_constraint(a, pltpu.HBM) for a in operands))
 
 
 def solution(mesh):

time: 112 us -> 110 us (0.982)
  Pallas kernels: 109 us -> 107 us
  local copies, waits for them, and re-layouts: 2.3 us -> 0.97 us
    unnamed x1, local copies, waits for them, and re-layouts: 2.3 us -> 0.97 us
    pallas_call x1, Pallas kernels: 109 us -> 107 us  [per_device(): pl.pallas_call(kernel, out_shape=jax.ShapeDtypeStruct(estimate.shape, f32...]
where the time goes in v4:
time: 110 us; the launch traced here: 108 us
  Pallas kernels  107 us (97%)
    pallas_call x1, Pallas kernels, per_device(): pl.pallas_call(kernel, out_shape=jax.ShapeDtypeStruct(estimate.shape, f32...  107 us

profile of v4, /device:TPU:24, one launch (start us, length us, event | category | flops | bytes accessed | tf_op | source)
XLA Modules:
  0.0 108.4 jit_solution(12168524346601950977)
XLA Ops:
  0.0 107.4 %deconvolve.1 = f32[1,128,2048]{2,1,0:T(8,128)S(1)} custom-call(f32[1,128,2048]{2,1,0:T(8,128)} %est_ref.1, f32[1,8,128,2048]{3,2,1,0:T(8,128)} %views_ref.1, f32[8,2,65]{2,1,0:T(2,128)} %psf_ref.1, s32[2,8]{1,0:T(2,128)} %bitcast.2, s32[2,8]{1,0:T(2,128)} %bitcast.3), custom_call_target="tpu_custom_call" | custom-call | tf_op jit(solution)/shard_map/deconvolve/pallas_call | solution.py:393
  107.4 1.0 copy.7

commit v5 on v4

--- a/solution.py
+++ b/solution.py
@@ -361,13 +361,16 @@
             if item[1:] == (CHUNKS - 1, 0):
                 halo(0).wait_send()
                 halo(1).wait_send()
-                for c in range(CHUNKS - 4):
+                for c in range(CHUNKS - 2):
                     sent(c)
             if item[1:] == (CHUNKS - 1, 3):
                 edge(0).wait_recv()
                 edge(1).wait_recv()
                 acc[REACH : 2 * REACH, :] += edges[0]
                 acc[TILE : REACH + TILE, :] += edges[1]
+                edge(0).wait_send()
+                edge(1).wait_send()
+                sent(CHUNKS - 2)
             back_y(*item[1:])
         elif item[0] == "edge":
             edge(0).start()
@@ -377,10 +380,7 @@
         else:
             last_x(item[2])
 
-    edge(0).wait_send()
-    edge(1).wait_send()
-    for c in range(CHUNKS - 4, CHUNKS):
-        sent(c)
+    sent(CHUNKS - 1)
 
 
 def per_device(estimate, views, psf, offsets, lengths):

time: 110 us -> 110 us (level)
  no operation moved by 1% of the time
where the time goes in v5:
time: 110 us; the launch traced here: 108 us
  Pallas kernels  107 us (97%)
    pallas_call x1, Pallas kernels, per_device(): pl.pallas_call(kernel, out_shape=jax.ShapeDtypeStruct(estimate.shape, f32...  107 us

profile of v5, /device:TPU:24, one launch (start us, length us, event | category | flops | bytes accessed | tf_op | source)
XLA Modules:
  0.0 108.3 jit_solution(15858015512202358054)
XLA Ops:
  0.0 107.3 %deconvolve.1 = f32[1,128,2048]{2,1,0:T(8,128)S(1)} custom-call(f32[1,128,2048]{2,1,0:T(8,128)} %est_ref.1, f32[1,8,128,2048]{3,2,1,0:T(8,128)} %views_ref.1, f32[8,2,65]{2,1,0:T(2,128)} %psf_ref.1, s32[2,8]{1,0:T(2,128)} %bitcast.2, s32[2,8]{1,0:T(2,128)} %bitcast.3), custom_call_target="tpu_custom_call" | custom-call | tf_op jit(solution)/shard_map/deconvolve/pallas_call | solution.py:393
  107.4 1.0 copy.7
